TPU v7x, 32 devices: a whole 2x2x4 slice. The times are simulated.
32 devices in a mesh: groups: 2 (over x), seq: 8 (over z, y), head: 2 (over core).
Axes of the slice: x: 2, y: 2, z: 4, core: 2. Of those that a mesh axis runs over, the one named last changes fastest.
Arguments:
- queries: bfloat16 [8192, 2048], P(('groups', 'seq'), 'head'), parts along dimension 0, may hold values from -6 to 6
- keys: bfloat16 [8192, 1024], P(('groups', 'seq'), 'head'), parts along dimension 0, may hold values from -6 to 6
- values: bfloat16 [8192, 1024], P(('groups', 'seq'), 'head'), parts along dimension 0, may hold values from -6 to 6
- segments: int32 [8192], P('groups'), parts along dimension 0, may hold values from 0 to 7, never falling along the last dimension, each value on 1 to 1024 neighbouring positions
- out_weight: bfloat16 [2048, 5376], P('head'), may hold values from -0.125 to 0.125
Outputs:
- mixed: bfloat16 [8192, 5376], P(('groups', 'seq')), parts along dimension 0
There are 2 independent parts, one for each index of `groups`. A program takes and returns all parts, laid end to end along the dimension named above; an argument that names none is the same for every part. Nothing has to cross between parts.
Inputs may be any that keep to these rules, and one draw needn't show every extreme that they name: `segments`: document ids never fall along the slab; each document has 1 to 1024 tokens, one exactly 1024.
All inputs are finite; a program needn't handle non-finite values.
Results may differ from a plain program's by a relative error of at most 0.011.
Values may be sent and summed in bfloat16 or wider, within the bound.
A program may use at most 128 MiB of HBM per device.

v0:
```python
import math
import jax
import jax.numpy as jnp
from jax import lax
from jax.sharding import PartitionSpec as P

HEAD_SIZE = 128
SCALAR = 168
ATTENTION_SPAN = 1024
HALO = 2


def from_behind(value, axis, by):
    peers = lax.axis_size(axis)
    pairs = [(i, i + by) for i in range(peers) if 0 <= i + by < peers]
    return lax.ppermute(value, axis, pairs)


def shards(queries, keys, values, segments, out_weight):
    tok_rows = queries.shape[0]
    heads_kv = keys.shape[1] // HEAD_SIZE
    query_group = queries.shape[1] // keys.shape[1]
    seq_index = lax.axis_index("seq")
    pieces = []
    for distance in range(HALO, 0, -1):
        pieces.append(from_behind((keys, values), "seq", distance))
    keys_ext = jnp.concatenate([piece[0] for piece in pieces] + [keys], axis=0)
    values_ext = jnp.concatenate([piece[1] for piece in pieces] + [values], axis=0)
    window_span = keys_ext.shape[0]
    first_row = seq_index * tok_rows
    pad_segments = jnp.concatenate([jnp.full((HALO * tok_rows,), -1, jnp.int32), segments])
    seg_key = lax.dynamic_slice_in_dim(pad_segments, first_row, window_span, 0)
    seg_query = lax.dynamic_slice_in_dim(segments, first_row, tok_rows, 0)
    key_pos = first_row - HALO * tok_rows + jnp.arange(window_span, dtype=jnp.int32)
    key_mat = keys_ext.reshape(window_span, heads_kv, HEAD_SIZE)
    value_mat = values_ext.reshape(window_span, heads_kv, HEAD_SIZE)
    token_block = math.gcd(tok_rows, 512)

    def one_block(block_id):
        start = block_id * token_block
        query_block = queries.reshape(token_block, heads_kv, query_group, HEAD_SIZE)
        query_pos = first_row + start + jnp.arange(token_block, dtype=jnp.int32)
        allowed = (
            (key_pos[None, :] <= query_pos[:, None])
            & (query_pos[:, None] - key_pos[None, :] < ATTENTION_SPAN)
            & (seg_key[None, :] == seg_query[:, None])
        )
        scores = jnp.einsum(
            "qkgd,pkd->kgqp", query_block, key_mat, preferred_element_type=jnp.float32
        ) * SCALAR ** (-0.5)
        masked = jnp.where(allowed, scores, -1e30)
        row_max = jnp.max(masked, axis=-1, keepdims=True)
        expo = jnp.where(allowed, jnp.exp(masked - row_max), 0.0)
        weights = (expo / jnp.sum(expo, axis=-1, keepdims=True)).astype(jnp.bfloat16)
        heads_out = jnp.einsum(
            "kgqp,pkd->qkgd", weights, value_mat, preferred_element_type=jnp.float32
        )
        return heads_out.astype(jnp.bfloat16).reshape(
            token_block, heads_kv * query_group * HEAD_SIZE
        )

    attended = lax.map(one_block, jnp.arange(tok_rows // token_block, dtype=jnp.int32)).reshape(
        tok_rows, -1
    )
    partial_terms = jnp.dot(attended, out_weight, preferred_element_type=jnp.float32)
    mixed = lax.psum(partial_terms, "head").astype(jnp.bfloat16)
    return mixed


def solution(mesh):
    placed = (
        P(("groups", "seq"), "head"),
        P(("groups", "seq"), "head"),
        P(("groups", "seq"), "head"),
        P("groups"),
        P("head", None),
    )
    return jax.shard_map(
        shards, mesh=mesh, in_specs=placed, out_specs=P(("groups", "seq"), None), check_vma=False
    )
```

profile of v0, /device:TPU:17, one launch (start us, length us, event | category | flops | bytes accessed | tf_op | source)
XLA Modules:
  0.0 131.4 jit_solution(17479699707473325721)
XLA Ops:
  0.0 1.3 copy.10
  1.3 3.1 %collective-permute-start.3 = (bf16[512,512]{0,1:T(8,128)(2,1)S(1)}, bf16[512,512]{0,1:T(8,128)(2,1)}, u32[]{:S(2)}, u32[]{:S(2)}) collective-permute-start(bf16[512,512]{0,1:T(8,128)(2,1)S(1)} %copy.10), channel_id=1, source_target_pairs={{0,2},{2,4},{4,6},{6,8},{8,10},{10,12},{12,14},{1,3},{3,5},{5,7},{... | collective-permute-start | bytes 1572872 | tf_op jit(solution)/shard_map/ppermute | solution.py:16
  4.4 3.2 %collective-permute-start.2 = (bf16[512,512]{0,1:T(8,128)(2,1)S(1)}, bf16[512,512]{0,1:T(8,128)(2,1)}, u32[]{:S(2)}, u32[]{:S(2)}) collective-permute-start(bf16[512,512]{0,1:T(8,128)(2,1)S(1)} %copy.10), channel_id=1, source_target_pairs={{0,4},{2,6},{4,8},{6,10},{8,12},{10,14},{1,5},{3,7},{5,9},{7,11},{... | collective-permute-start | bytes 1572872 | tf_op jit(solution)/shard_map/ppermute | solution.py:16
  7.6 1.9 %collective-permute-start = (bf16[512,512]{1,0:T(8,128)(2,1)}, bf16[512,512]{1,0:T(8,128)(2,1)S(1)}, u32[]{:S(2)}, u32[]{:S(2)}) collective-permute-start(bf16[512,512]{1,0:T(8,128)(2,1)} %param.7), channel_id=1, source_target_pairs={{0,4},{2,6},{4,8},{6,10},{8,12},{10,14},{1,5},{3,7},{5,9},{7,11},{... | collective-permute-start | bytes 1572872 | tf_op jit(solution)/shard_map/ppermute | solution.py:16
  9.6 1.9 %collective-permute-start.1 = (bf16[512,512]{1,0:T(8,128)(2,1)}, bf16[512,512]{1,0:T(8,128)(2,1)}, u32[]{:S(2)}, u32[]{:S(2)}) collective-permute-start(bf16[512,512]{1,0:T(8,128)(2,1)} %param.7), channel_id=1, source_target_pairs={{0,2},{2,4},{4,6},{6,8},{8,10},{10,12},{12,14},{1,3},{3,5},{5,7},{... | collective-permute-start | bytes 1572872 | tf_op jit(solution)/shard_map/ppermute | solution.py:16
  11.5 0.8 pad_dynamic-slice_fusion
  12.3 0.8 dynamic_slice.10
  13.1 1.9 %fusion.9 = pred[512,1536]{0,1:T(8,128)(4,1)} fusion(s32[512]{0:T(512)S(1)} %dynamic_slice.10, s32[512]{0:T(512)S(1)} %iota_add_fusion.1, s32[1536]{0:T(1024)S(1)} %get-tuple-element.21, s32[1536]{0:T(1024)S(1)} %get-tuple-element.22), kind=kLoop, calls=%fused_computation.12 | loop fusion | flops 4718592 | bytes 802816 | tf_op jit(solution)/shard_map/while/body/eval_jaxpr/and | solution.py:44
  14.9 1.8 %reshape.31 = bf16[512,4,2,128]{3,2,1,0:T(2,128)(2,1)S(1)} reshape(bf16[512,1024]{1,0:T(8,128)(2,1)} %param.5) | data formatting | bytes 2097152 | tf_op jit(solution)/shard_map/while/body/eval_jaxpr/reshape | solution.py:41
  16.7 0.0 copy-start.1
  16.7 13.3 %collective-permute-done = bf16[512,512]{1,0:T(8,128)(2,1)S(1)} collective-permute-done((bf16[512,512]{1,0:T(8,128)(2,1)}, bf16[512,512]{1,0:T(8,128)(2,1)S(1)}, u32[]{:S(2)}, u32[]{:S(2)}) %collective-permute-start) | collective-permute-done | bytes 524320 | tf_op jit(solution)/shard_map/ppermute | solution.py:16
  30.1 0.0 copy-start.2
  30.1 0.8 copy-done.2
  30.9 19.8 %collective-permute-done.1 = bf16[512,512]{1,0:T(8,128)(2,1)} collective-permute-done((bf16[512,512]{1,0:T(8,128)(2,1)}, bf16[512,512]{1,0:T(8,128)(2,1)}, u32[]{:S(2)}, u32[]{:S(2)}) %collective-permute-start.1) | collective-permute-done | bytes 524320 | tf_op jit(solution)/shard_map/ppermute | solution.py:16
  50.7 1.5 %pad_maximum_fusion = bf16[1536,512]{1,0:T(8,128)(2,1)S(1)} fusion(bf16[512,512]{1,0:T(8,128)(2,1)} %param.7, bf16[512,512]{1,0:T(8,128)(2,1)} %collective-permute-done.1, bf16[512,512]{1,0:T(8,128)(2,1)} %copy-done.2), kind=kLoop, calls=%fused_computation.13 | loop fusion | flops 4718592 | bytes 3145728 | tf_op jit(solution)/shard_map/concatenate | solution.py:28
  52.1 1.6 %copy.9 = bf16[1536,512]{0,1:T(8,128)(2,1)} copy(bf16[1536,512]{1,0:T(8,128)(2,1)S(1)} %pad_maximum_fusion) | data formatting | bytes 3145728 | tf_op jit(solution)/shard_map/concatenate | solution.py:28
  53.7 0.0 collective-permute-done.3
  53.7 0.0 collective-permute-done.2
  53.7 2.5 %pad_maximum_fusion.1 = bf16[1536,512]{0,1:T(8,128)(2,1)} fusion(bf16[512,512]{0,1:T(8,128)(2,1)S(1)} %copy.10, bf16[512,512]{0,1:T(8,128)(2,1)} %collective-permute-done.3, bf16[512,512]{0,1:T(8,128)(2,1)} %collective-permute-done.2), kind=kLoop, calls=%fused_computation.14 | loop fusion | flops 4718592 | bytes 3145728 | tf_op jit(solution)/shard_map/concatenate | solution.py:27
  56.2 0.0 copy-done.1
  56.2 0.0 copy-start
  56.2 13.4 %fusion.28 = f32[4,2,512]{2,1,0:T(2,128)S(1)} fusion(pred[512,1536]{0,1:T(8,128)(4,1)} %fusion.9, bf16[1536,4,128,1]{0,2,3,1:T(8,128)(2,1)} %bitcast.32, bf16[512,4,2,128]{3,2,1,0:T(2,128)(2,1)S(1)} %reshape.31), kind=kOutput, calls=%fused_computation.29 | convolution fusion | flops 1642071552 | bytes 3424256 | tf_op jit(solution)/shard_map/while/body/eval_jaxpr/sub | solution.py:53
  69.6 0.0 copy-done
  69.6 15.7 %fusion.10 = bf16[4,128,2,512]{3,1,2,0:T(8,128)(2,1)S(1)} fusion(bf16[1536,4,128,1]{0,2,3,1:T(8,128)(2,1)S(1)} %bitcast.31, f32[4,2,512]{2,1,0:T(2,128)S(1)} %fusion.28, pred[512,1536]{0,1:T(8,128)(4,1)} %fusion.9, bf16[1536,4,128,1]{0,2,3,1:T(8,128)(2,1)} %bitcast.33, bf16[512,4,2,128]{3,2,1,0:T(2,128)(2,1)} %copy-done.1), kind=kOutput, calls=%fused_computation.15 | convolution fusion | flops 3259504128 | bytes 6045696 | tf_op jit(solution)/shard_map/while/body/eval_jaxpr/kgqp,pkd->qkgd/dot_general | solution.py:55
  85.4 12.7 %fusion.31 = f32[512,5376]{1,0:T(8,128)} fusion(bf16[512,1024]{0,1:T(8,128)(2,1)S(1)} %bitcast.34, bf16[1024,5376]{1,0:T(8,128)(2,1)} %param.9), kind=kOutput, calls=%fused_computation.30 | convolution fusion | flops 5637144576 | bytes 23068672 | tf_op jit(solution)/shard_map/dot_general | solution.py:65
  98.1 33.3 %all-reduce.2 = bf16[512,5376]{1,0:T(8,128)(2,1)} all-reduce(f32[512,5376]{1,0:T(8,128)} %fusion.31), channel_id=1, replica_groups=mesh['groups'=2,'seq'=8,'head'=2] {'head'}, use_global_device_ids=true, to_apply=%region_2.3 | all-reduce | flops 2752512 | bytes 16515072 | tf_op jit(solution)/shard_map/psum | solution.py:66
  (1 shorter events, 0.0 us)
Async XLA Ops:
  1.3 52.5 %collective-permute-start.3 = (bf16[512,512]{0,1:T(8,128)(2,1)S(1)}, bf16[512,512]{0,1:T(8,128)(2,1)}, u32[]{:S(2)}, u32[]{:S(2)}) collective-permute-start(bf16[512,512]{0,1:T(8,128)(2,1)S(1)} %copy.10), channel_id=1, source_target_pairs={{0,2},{2,4},{4,6},{6,8},{8,10},{10,12},{12,14},{1,3},{3,5},{5,7},{... | collective-permute-start | bytes 1572872 | tf_op jit(solution)/shard_map/ppermute | solution.py:16
  4.4 49.3 %collective-permute-start.2 = (bf16[512,512]{0,1:T(8,128)(2,1)S(1)}, bf16[512,512]{0,1:T(8,128)(2,1)}, u32[]{:S(2)}, u32[]{:S(2)}) collective-permute-start(bf16[512,512]{0,1:T(8,128)(2,1)S(1)} %copy.10), channel_id=1, source_target_pairs={{0,4},{2,6},{4,8},{6,10},{8,12},{10,14},{1,5},{3,7},{5,9},{7,11},{... | collective-permute-start | bytes 1572872 | tf_op jit(solution)/shard_map/ppermute | solution.py:16
  7.6 22.4 %collective-permute-start = (bf16[512,512]{1,0:T(8,128)(2,1)}, bf16[512,512]{1,0:T(8,128)(2,1)S(1)}, u32[]{:S(2)}, u32[]{:S(2)}) collective-permute-start(bf16[512,512]{1,0:T(8,128)(2,1)} %param.7), channel_id=1, source_target_pairs={{0,4},{2,6},{4,8},{6,10},{8,12},{10,14},{1,5},{3,7},{5,9},{7,11},{... | collective-permute-start | bytes 1572872 | tf_op jit(solution)/shard_map/ppermute | solution.py:16
  9.6 41.1 %collective-permute-start.1 = (bf16[512,512]{1,0:T(8,128)(2,1)}, bf16[512,512]{1,0:T(8,128)(2,1)}, u32[]{:S(2)}, u32[]{:S(2)}) collective-permute-start(bf16[512,512]{1,0:T(8,128)(2,1)} %param.7), channel_id=1, source_target_pairs={{0,2},{2,4},{4,6},{6,8},{8,10},{10,12},{12,14},{1,3},{3,5},{5,7},{... | collective-permute-start | bytes 1572872 | tf_op jit(solution)/shard_map/ppermute | solution.py:16
  16.7 39.4 %copy-start.1 = (bf16[512,4,2,128]{3,2,1,0:T(2,128)(2,1)}, bf16[512,4,2,128]{3,2,1,0:T(2,128)(2,1)S(1)}, u32[]{:S(2)}) copy-start(bf16[512,4,2,128]{3,2,1,0:T(2,128)(2,1)S(1)} %reshape.31) | copy-start | bytes 3145732
  30.1 0.8 copy-start.2
  56.2 13.4 %copy-start = (bf16[1536,512]{0,1:T(8,128)(2,1)S(1)}, bf16[1536,512]{0,1:T(8,128)(2,1)}, u32[]{:S(2)}) copy-start(bf16[1536,512]{0,1:T(8,128)(2,1)} %copy.9) | copy-start | bytes 4718596
where the time goes:
time: 132 us; the launch traced here: 131 us
  matrix products  41.9 us (32%)
  blocking collectives  33.3 us (25%)
  waiting for transfers between devices  33.1 us (25%)
  starting transfers between devices  10.2 us (8%)
  other arithmetic  6.6 us (5%)
  local copies, waits for them, and re-layouts  6.17 us (5%)
    psum x1, blocking collectives, shards(): mixed = lax.psum(partial_terms, 'head').astype(jnp.bfloat16)  33.3 us
    ppermute x4, waiting for transfers between devices, from_behind(): return lax.ppermute(value, axis, pairs)  33.1 us
    dot_general x1, matrix products, one_block(): jnp.einsum('kgqp,pkd->qkgd', weights, value_mat, preferred_element_type=j...  15.7 us
    sub x1, matrix products, one_block(): expo = jnp.where(allowed, jnp.exp(masked - row_max), 0.0)  13.4 us
    dot_general x1, matrix products, shards(): jnp.dot(attended, out_weight, preferred_element_type=jnp.float32)  12.7 us
    ppermute x4, starting transfers between devices, from_behind(): return lax.ppermute(value, axis, pairs)  10.2 us
  transfers between devices with their start and end apart: 4, of which 2 were waited for; matrix products, arithmetic and copies ran while one was open for 6% of the time, Pallas kernels for 0%

commit v1 on v0

--- a/solution.py
+++ b/solution.py
@@ -8,6 +8,11 @@
 SCALAR = 168
 ATTENTION_SPAN = 1024
 HALO = 2
+
+
+def spots_drive(shard_in, axis_name):
+    b_now = jax.lax.all_gather(shard_in, axis_name).sum(axis=0)
+    return b_now
 
 
 def from_behind(value, axis, by):
@@ -63,7 +68,7 @@
         tok_rows, -1
     )
     partial_terms = jnp.dot(attended, out_weight, preferred_element_type=jnp.float32)
-    mixed = lax.psum(partial_terms, "head").astype(jnp.bfloat16)
+    mixed = spots_drive(partial_terms, "head").astype(jnp.bfloat16)
     return mixed
 
 

time: 132 us -> 163 us (1.23)
  waiting for transfers between devices: 33.1 us -> 70.9 us
  blocking collectives: 33.3 us -> 0 us
  between operations: 0.09 us -> 13.5 us
  other arithmetic: 6.6 us -> 17.8 us
  local copies, waits for them, and re-layouts: 6.17 us -> 7.85 us
    all_gather x0 -> x1, waiting for transfers between devices: none -> 38.5 us  [spots_drive(): b_now = jax.lax.all_gather(shard_in, axis_name).sum(axis=0)]
    psum x1 -> x0, blocking collectives: 33.3 us -> none  [shards(): mixed = lax.psum(partial_terms, 'head').astype(jnp.bfloat16)]
    reduce_sum x0 -> x1, other arithmetic: none -> 12.5 us  [spots_drive(): b_now = jax.lax.all_gather(shard_in, axis_name).sum(axis=0)]
  transfers between devices with their start and end apart: 4 -> 5, of which waited for: 2 -> 3; matrix products, arithmetic and copies ran while one was open for 6% -> 6% of each run, Pallas kernels for 0% -> 0%
where the time goes in v1:
time: 163 us; the launch traced here: 161 us
  waiting for transfers between devices  70.9 us (43%)
  matrix products  41.2 us (25%)
  other arithmetic  17.8 us (11%)
  between operations  13.5 us (8%)
  starting transfers between devices  10.2 us (6%)
  local copies, waits for them, and re-layouts  7.85 us (5%)
    all_gather x1, waiting for transfers between devices, spots_drive(): b_now = jax.lax.all_gather(shard_in, axis_name).sum(axis=0)  38.5 us
    ppermute x4, waiting for transfers between devices, from_behind(): return lax.ppermute(value, axis, pairs)  32.4 us
    dot_general x1, matrix products, one_block(): jnp.einsum('kgqp,pkd->qkgd', weights, value_mat, preferred_element_type=j...  16.3 us
    dot_general x1, matrix products, shards(): jnp.dot(attended, out_weight, preferred_element_type=jnp.float32)  12.8 us
    reduce_sum x1, other arithmetic, spots_drive(): b_now = jax.lax.all_gather(shard_in, axis_name).sum(axis=0)  12.5 us
    sub x1, matrix products, one_block(): expo = jnp.where(allowed, jnp.exp(masked - row_max), 0.0)  12.1 us
    ppermute x4, starting transfers between devices, from_behind(): return lax.ppermute(value, axis, pairs)  10.2 us
  transfers between devices with their start and end apart: 5, of which 3 were waited for; matrix products, arithmetic and copies ran while one was open for 6% of the time, Pallas kernels for 0%

profile of v1, /device:TPU:17, one launch (start us, length us, event | category | flops | bytes accessed | tf_op | source)
XLA Modules:
  0.0 161.4 jit_solution(18055654217611041493)
XLA Ops:
  6.5 0.0 copy-start.1
  6.5 0.0 all-gather.3.cloned.1.call-start
  6.5 1.3 copy.10
  7.9 3.1 %collective-permute-start.3 = (bf16[512,512]{0,1:T(8,128)(2,1)S(1)}, bf16[512,512]{0,1:T(8,128)(2,1)S(1)}, u32[]{:S(2)}, u32[]{:S(2)}) collective-permute-start(bf16[512,512]{0,1:T(8,128)(2,1)S(1)} %copy.10), channel_id=1, source_target_pairs={{0,2},{2,4},{4,6},{6,8},{8,10},{10,12},{12,14},{1,3},{3,5},{5,7},{... | collective-permute-start | bytes 1572872 | tf_op jit(solution)/shard_map/ppermute | solution.py:21
  11.0 3.2 %collective-permute-start.2 = (bf16[512,512]{0,1:T(8,128)(2,1)S(1)}, bf16[512,512]{0,1:T(8,128)(2,1)}, u32[]{:S(2)}, u32[]{:S(2)}) collective-permute-start(bf16[512,512]{0,1:T(8,128)(2,1)S(1)} %copy.10), channel_id=1, source_target_pairs={{0,4},{2,6},{4,8},{6,10},{8,12},{10,14},{1,5},{3,7},{5,9},{7,11},{... | collective-permute-start | bytes 1572872 | tf_op jit(solution)/shard_map/ppermute | solution.py:21
  14.2 1.9 %collective-permute-start = (bf16[512,512]{1,0:T(8,128)(2,1)}, bf16[512,512]{1,0:T(8,128)(2,1)S(1)}, u32[]{:S(2)}, u32[]{:S(2)}) collective-permute-start(bf16[512,512]{1,0:T(8,128)(2,1)} %param.7), channel_id=1, source_target_pairs={{0,4},{2,6},{4,8},{6,10},{8,12},{10,14},{1,5},{3,7},{5,9},{7,11},{... | collective-permute-start | bytes 1572872 | tf_op jit(solution)/shard_map/ppermute | solution.py:21
  16.2 1.9 %collective-permute-start.1 = (bf16[512,512]{1,0:T(8,128)(2,1)}, bf16[512,512]{1,0:T(8,128)(2,1)}, u32[]{:S(2)}, u32[]{:S(2)}) collective-permute-start(bf16[512,512]{1,0:T(8,128)(2,1)} %param.7), channel_id=1, source_target_pairs={{0,2},{2,4},{4,6},{6,8},{8,10},{10,12},{12,14},{1,3},{3,5},{5,7},{... | collective-permute-start | bytes 1572872 | tf_op jit(solution)/shard_map/ppermute | solution.py:21
  18.1 0.8 pad_dynamic-slice_fusion
  18.9 0.8 dynamic_slice.10
  19.6 1.9 %fusion.9 = pred[512,1536]{0,1:T(8,128)(4,1)} fusion(s32[512]{0:T(512)S(1)} %dynamic_slice.10, s32[512]{0:T(512)S(1)} %iota_add_fusion.1, s32[1536]{0:T(1024)S(1)} %get-tuple-element.21, s32[1536]{0:T(1024)S(1)} %get-tuple-element.22), kind=kLoop, calls=%fused_computation.12 | loop fusion | flops 4718592 | bytes 802816 | tf_op jit(solution)/shard_map/while/body/eval_jaxpr/and | solution.py:49
  21.5 2.6 %reshape.31 = bf16[512,4,2,128]{3,2,1,0:T(2,128)(2,1)} reshape(bf16[512,1024]{1,0:T(8,128)(2,1)} %param.5) | data formatting | bytes 2097152 | tf_op jit(solution)/shard_map/while/body/eval_jaxpr/reshape | solution.py:46
  24.1 12.6 %collective-permute-done = bf16[512,512]{1,0:T(8,128)(2,1)S(1)} collective-permute-done((bf16[512,512]{1,0:T(8,128)(2,1)}, bf16[512,512]{1,0:T(8,128)(2,1)S(1)}, u32[]{:S(2)}, u32[]{:S(2)}) %collective-permute-start) | collective-permute-done | bytes 524320 | tf_op jit(solution)/shard_map/ppermute | solution.py:21
  36.7 0.0 copy-start.3
  36.7 0.8 copy-done.3
  37.5 19.8 %collective-permute-done.1 = bf16[512,512]{1,0:T(8,128)(2,1)} collective-permute-done((bf16[512,512]{1,0:T(8,128)(2,1)}, bf16[512,512]{1,0:T(8,128)(2,1)}, u32[]{:S(2)}, u32[]{:S(2)}) %collective-permute-start.1) | collective-permute-done | bytes 524320 | tf_op jit(solution)/shard_map/ppermute | solution.py:21
  57.3 0.0 copy-done.1
  57.3 1.3 pad_maximum_fusion
  58.6 1.6 copy.9
  60.1 0.0 collective-permute-done.3
  60.1 0.0 copy-start.2
  60.2 0.8 copy-done.2
  61.0 0.0 collective-permute-done.2
  61.0 1.3 pad_maximum_fusion.1
  62.3 0.0 copy-start
  62.3 12.1 %fusion.28 = f32[4,2,512]{2,1,0:T(2,128)S(1)} fusion(pred[512,1536]{0,1:T(8,128)(4,1)} %fusion.9, bf16[1536,4,128,1]{0,2,3,1:T(8,128)(2,1)S(1)} %bitcast.34, bf16[512,4,2,128]{3,2,1,0:T(2,128)(2,1)} %reshape.31), kind=kOutput, calls=%fused_computation.29 | convolution fusion | flops 1642071552 | bytes 3424256 | tf_op jit(solution)/shard_map/while/body/eval_jaxpr/sub | solution.py:58
  74.4 0.0 copy-done
  74.4 16.3 %fusion.10 = bf16[4,128,2,512]{3,1,2,0:T(8,128)(2,1)} fusion(bf16[1536,4,128,1]{0,2,3,1:T(8,128)(2,1)S(1)} %bitcast.33, f32[4,2,512]{2,1,0:T(2,128)S(1)} %fusion.28, pred[512,1536]{0,1:T(8,128)(4,1)} %fusion.9, bf16[1536,4,128,1]{0,2,3,1:T(8,128)(2,1)S(1)} %bitcast.35, bf16[512,4,2,128]{3,2,1,0:T(2,128)(2,1)} %reshape.31), kind=kOutput, calls=%fused_computation.15 | convolution fusion | flops 3259504128 | bytes 6045696 | tf_op jit(solution)/shard_map/while/body/eval_jaxpr/kgqp,pkd->qkgd/dot_general | solution.py:60
  90.7 12.8 %fusion.31 = f32[512,5376]{1,0:T(8,128)} fusion(bf16[512,1024]{0,1:T(8,128)(2,1)} %bitcast.36, bf16[1024,5376]{1,0:T(8,128)(2,1)} %param.9), kind=kOutput, calls=%fused_computation.30 | convolution fusion | flops 5637144576 | bytes 23068672 | tf_op jit(solution)/shard_map/dot_general | solution.py:70
  103.5 0.0 all-gather.3.cloned.1.call-update
  103.6 38.5 %all-gather.3.cloned.1.call-done = f32[1024,5376]{1,0:T(8,128)} async-done(((f32[512,5376]{1,0:T(8,128)}), f32[1024,5376]{1,0:T(8,128)}) %all-gather.3.cloned.1.call-update) | async-done | bytes 22020112 | tf_op jit(solution)/shard_map/all_gather | solution.py:14
  142.1 12.5 %reduce_sum.20 = bf16[512,5376]{1,0:T(8,128)(2,1)} reduce(f32[2,512,5376]{2,1,0:T(8,128)} %bitcast.32, f32[]{:T(128)} %constant.47.clone.1), dimensions={0}, to_apply=%region_2.3 | reduce | flops 2752512 | bytes 27525124 | tf_op jit(solution)/shard_map/reduce_sum | solution.py:14
  (1 shorter events, 0.0 us)
Async XLA Ops:
  6.5 50.7 %copy-start.1 = (bf16[512,512]{1,0:T(8,128)(2,1)S(1)}, bf16[512,512]{1,0:T(8,128)(2,1)}, u32[]{:S(2)}) copy-start(bf16[512,512]{1,0:T(8,128)(2,1)} %param.7) | copy-start | bytes 1572868
  6.5 135.5 %all-gather.3.cloned.1.call-start = ((), (), s32[]{:S(2)}) async-start(), calls=%async_computation | async-start | bytes 33030144 | tf_op jit(solution)/shard_map/all_gather | solution.py:14
  7.9 52.3 %collective-permute-start.3 = (bf16[512,512]{0,1:T(8,128)(2,1)S(1)}, bf16[512,512]{0,1:T(8,128)(2,1)S(1)}, u32[]{:S(2)}, u32[]{:S(2)}) collective-permute-start(bf16[512,512]{0,1:T(8,128)(2,1)S(1)} %copy.10), channel_id=1, source_target_pairs={{0,2},{2,4},{4,6},{6,8},{8,10},{10,12},{12,14},{1,3},{3,5},{5,7},{... | collective-permute-start | bytes 1572872 | tf_op jit(solution)/shard_map/ppermute | solution.py:21
  11.0 50.0 %collective-permute-start.2 = (bf16[512,512]{0,1:T(8,128)(2,1)S(1)}, bf16[512,512]{0,1:T(8,128)(2,1)}, u32[]{:S(2)}, u32[]{:S(2)}) collective-permute-start(bf16[512,512]{0,1:T(8,128)(2,1)S(1)} %copy.10), channel_id=1, source_target_pairs={{0,4},{2,6},{4,8},{6,10},{8,12},{10,14},{1,5},{3,7},{5,9},{7,11},{... | collective-permute-start | bytes 1572872 | tf_op jit(solution)/shard_map/ppermute | solution.py:21
  14.2 22.4 %collective-permute-start = (bf16[512,512]{1,0:T(8,128)(2,1)}, bf16[512,512]{1,0:T(8,128)(2,1)S(1)}, u32[]{:S(2)}, u32[]{:S(2)}) collective-permute-start(bf16[512,512]{1,0:T(8,128)(2,1)} %param.7), channel_id=1, source_target_pairs={{0,4},{2,6},{4,8},{6,10},{8,12},{10,14},{1,5},{3,7},{5,9},{7,11},{... | collective-permute-start | bytes 1572872 | tf_op jit(solution)/shard_map/ppermute | solution.py:21
  16.2 41.1 %collective-permute-start.1 = (bf16[512,512]{1,0:T(8,128)(2,1)}, bf16[512,512]{1,0:T(8,128)(2,1)}, u32[]{:S(2)}, u32[]{:S(2)}) collective-permute-start(bf16[512,512]{1,0:T(8,128)(2,1)} %param.7), channel_id=1, source_target_pairs={{0,2},{2,4},{4,6},{6,8},{8,10},{10,12},{12,14},{1,3},{3,5},{5,7},{... | collective-permute-start | bytes 1572872 | tf_op jit(solution)/shard_map/ppermute | solution.py:21
  36.7 0.8 copy-start.3
  60.1 0.8 copy-start.2
  62.3 12.2 %copy-start = (bf16[1536,512]{0,1:T(8,128)(2,1)S(1)}, bf16[1536,512]{0,1:T(8,128)(2,1)}, u32[]{:S(2)}) copy-start(bf16[1536,512]{0,1:T(8,128)(2,1)} %copy.9) | copy-start | bytes 4718596
Sparse Core Ops, SparseCore 0:
  103.7 38.3 all-gather.2
